TPU v7x, 256 devices: a whole 4x4x8 slice. The times are simulated.
256 devices in a mesh: ep: 64 (over z, x, y_hi), tp: 4 (over y_lo, core).
Axes of the slice: x: 4, y: 4 (y_hi: 2, y_lo: 2; y = y_hi * 2 + y_lo), z: 8, core: 2. Of those that a mesh axis runs over, the one named last changes fastest.
Arguments:
- context: bfloat16 [8192, 4096], P('ep', 'tp'), may hold values from -6 to 6
- wo_proj: bfloat16 [4096, 4096], P('tp'), may hold values from -0.09375 to 0.09375
- residual: bfloat16 [8192, 4096], P(('ep', 'tp')), may hold values from -16 to 16
- norm_gain: bfloat16 [4096], replicated, may hold values from 0.25 to 1.75
- expert_ids: int32 [8192, 8], P(('ep', 'tp')), may hold values from 0 to 63, all different within a row; in each aligned block of 32 rows (0 to 31, 32 to 63, ...) at most 8 rows name the same one
- route_weights: float32 [8192, 8], P(('ep', 'tp')), may hold values from 0.1 to 1
- w_gate_up: bfloat16 [64, 2, 768, 4096], P('ep', None, 'tp'), may hold values from -0.09375 to 0.09375
- w_down: bfloat16 [64, 768, 4096], P('ep', 'tp'), may hold values from -0.21875 to 0.21875
Outputs:
- layer_out: bfloat16 [8192, 4096], P(('ep', 'tp'))
Inputs may be any that keep to these rules, and one draw needn't show every extreme that they name: `expert_ids`: within the routes of one device's 32 tokens no expert is named more than 8 times, a bound that some block reaches; a token names 8 different experts.
All inputs are finite; a program needn't handle non-finite values.
Results may differ from a plain program's by a relative error of at most 0.0085.
Values may be sent and summed in bfloat16 or wider, within the bound.
A program may use at most 128 MiB of HBM per device.

v0:
```python
import jax
import jax.numpy as jnp
from jax import lax
from jax.sharding import PartitionSpec as P


def local(context, wo_proj, residual, norm_gain, expert_ids, route_weights, w_gate_up, w_down):
    quarter_rows, model_width = residual.shape
    top_count = expert_ids.shape[1]
    exp_local = w_gate_up.shape[0]
    ep_size = lax.axis_size("ep")
    experts = exp_local * ep_size
    capacity = max(2, min(quarter_rows, 2 * quarter_rows * top_count // experts))
    attn = lax.psum_scatter(
        jnp.dot(context, wo_proj, preferred_element_type=jnp.float32),
        "tp",
        scatter_dimension=0,
        tiled=True,
    )
    hidden = residual.astype(jnp.float32) + attn
    inverse_rms = lax.rsqrt(jnp.mean(hidden * hidden, axis=1, keepdims=True) + 1e-06)
    normed = (hidden * inverse_rms * norm_gain.astype(jnp.float32)).astype(jnp.bfloat16)
    flat_ids = expert_ids.reshape(-1)
    onehot = (flat_ids[:, None] == jnp.arange(experts, dtype=jnp.int32)[None, :]).astype(jnp.int32)
    before = jnp.cumsum(onehot, axis=0, dtype=jnp.int32) - onehot
    position = jnp.sum(before * onehot, axis=1, dtype=jnp.int32)
    slot_ids = flat_ids * capacity + position
    slot_range = jnp.arange(experts * capacity, dtype=jnp.int32)
    selected = slot_range[:, None] == slot_ids[None, :]
    placement = jnp.any(
        selected.reshape(experts * capacity, quarter_rows, top_count), axis=2
    ).astype(jnp.bfloat16)
    send_rows = jnp.dot(placement, normed, preferred_element_type=jnp.float32).astype(jnp.bfloat16)
    send_rows = send_rows.reshape(ep_size, exp_local * capacity, model_width)
    received = lax.all_to_all(send_rows, "ep", split_axis=0, concat_axis=0, tiled=True)
    received = received.reshape(ep_size, exp_local, capacity, model_width)
    piece = lax.all_gather(received[None], "tp", axis=0, tiled=True)
    gate = jnp.einsum(
        "nsjcd,jfd->nsjcf", piece, w_gate_up[:, 0], preferred_element_type=jnp.float32
    )
    up_proj = jnp.einsum(
        "nsjcd,jfd->nsjcf", piece, w_gate_up[:, 1], preferred_element_type=jnp.float32
    )
    activated = (jax.nn.silu(gate) * up_proj).astype(jnp.bfloat16)
    partials = jnp.einsum("nsjcf,jfd->nsjcd", activated, w_down, preferred_element_type=jnp.float32)
    combined = lax.psum_scatter(
        partials.astype(jnp.bfloat16), "tp", scatter_dimension=0, tiled=True
    ).astype(jnp.float32)
    expert_out = combined[0].astype(jnp.bfloat16)
    returned = lax.all_to_all(
        expert_out.reshape(ep_size, exp_local * capacity, model_width),
        "ep",
        split_axis=0,
        concat_axis=0,
        tiled=True,
    )
    returned = returned.reshape(experts * capacity, model_width)
    token_slots = slot_ids.reshape(quarter_rows, top_count)
    mixture = jnp.zeros((quarter_rows, model_width), jnp.float32)
    for choice_index in range(top_count):
        picker = (slot_range[None, :] == token_slots[:, choice_index][:, None]).astype(jnp.bfloat16)
        picked = jnp.dot(picker, returned, preferred_element_type=jnp.float32)
        mixture = mixture + route_weights[:, choice_index : choice_index + 1] * picked
    return (hidden + mixture).astype(jnp.bfloat16)


def solution(mesh):
    in_specs = (
        P("ep", "tp"),
        P("tp", None),
        P(("ep", "tp"), None),
        P(),
        P(("ep", "tp"), None),
        P(("ep", "tp"), None),
        P("ep", None, "tp", None),
        P("ep", "tp", None),
    )
    out_specs = P(("ep", "tp"), None)
    return jax.shard_map(local, mesh=mesh, in_specs=in_specs, out_specs=out_specs, check_vma=False)
```

profile of v0, /device:TPU:32, one launch (start us, length us, event | category | flops | bytes accessed | tf_op | source)
XLA Modules:
  0.0 636.2 jit_solution(903657910014447604)
XLA Ops:
  6.5 0.0 reduce-scatter.3.cloned.1.call-start
  6.6 6.2 fusion.50
  12.8 0.0 all-gather.3.cloned.1.call-start
  12.9 0.1 copy.22
  12.9 0.1 eq.164
  13.0 0.1 eq.160
  13.2 0.6 reduce-window.6
  13.8 0.2 slice_reduce_fusion
  14.0 0.1 fusion.39
  14.1 0.1 reduce_sum.21
  14.2 0.2 fusion.34
  14.5 31.8 %reduce-scatter.3.cloned.1.call-done = f32[32,4096]{1,0:T(8,128)} async-done(((f32[128,4096]{1,0:T(8,128)}), f32[32,4096]{1,0:T(8,128)}) %reduce-scatter.3.cloned.1.call-update) | async-done | bytes 524304 | tf_op jit(solution)/shard_map/reduce_scatter | solution.py:14
  46.2 1.2 multiply_reduce_fusion
  47.5 2.4 fusion
  49.8 109.7 %all_to_all.10 = bf16[64,8,4096]{2,1,0:T(8,128)(2,1)} all-to-all(bf16[64,8,4096]{2,1,0:T(8,128)(2,1)S(1)} %fusion), channel_id=1, replica_groups=mesh['ep'=64,'tp'=4] {'ep'}, dimensions={0} | all-to-all | bytes 8388608 | tf_op jit(solution)/shard_map/all_to_all | solution.py:35
  159.5 0.0 all-gather.3.cloned.1.call-update
  159.5 0.2 reduce-scatter.5.cloned.1.call-start
  159.8 147.1 %all-gather.3.cloned.1.call-done = bf16[256,8,4096]{2,1,0:T(8,128)(2,1)} async-done(((bf16[64,8,4096]{2,1,0:T(8,128)(2,1)}), bf16[256,8,4096]{2,1,0:T(8,128)(2,1)}) %all-gather.3.cloned.1.call-update) | async-done | bytes 16777232 | tf_op jit(solution)/shard_map/all_gather | solution.py:37
  306.9 12.2 %fusion.23 = f32[4,64,8,192]{3,2,1,0:T(8,128)} fusion(bf16[4,64,8,4096]{3,2,1,0:T(8,128)(2,1)} %bitcast.130, bf16[1,2,192,4096]{3,2,1,0:T(8,128)(2,1)} %param.14), kind=kOutput, calls=%fused_computation.36 | convolution fusion | flops 3221225472 | bytes 19922944 | tf_op jit(solution)/shard_map/nsjcd,jfd->nsjcf/dot_general | solution.py:41
  319.0 23.8 %convert_bitcast_fusion = bf16[4,64,1,8,4096]{4,3,1,0,2:T(8,128)(2,1)} fusion(bf16[1,192,4096]{2,1,0:T(8,128)(2,1)S(1)} %copy-done, f32[4,64,8,192]{3,2,1,0:T(8,128)} %fusion.23, bf16[4,64,8,4096]{3,2,1,0:T(8,128)(2,1)} %bitcast.131, bf16[1,2,192,4096]{3,2,1,0:T(8,128)(2,1)} %param.14), kind=kOutput, calls=%fused_computation | convolution fusion | flops 6453198848 | bytes 38797312 | tf_op jit(solution)/shard_map/nsjcf,jfd->nsjcd/dot_general | solution.py:45
  342.9 151.7 %reduce-scatter.5.cloned.1.call-done = bf16[1,64,1,8,4096]{4,3,1,0,2:T(8,128)(2,1)} async-done(((bf16[4,64,1,8,4096]{4,3,1,0,2:T(8,128)(2,1)}), bf16[1,64,1,8,4096]{4,3,1,0,2:T(8,128)(2,1)}) %reduce-scatter.5.cloned.1.call-update) | async-done | bytes 4194320 | tf_op jit(solution)/shard_map/reduce_scatter | solution.py:46
  494.6 12.9 %all-to-all-start.1 = ((bf16[64,8,4096]{2,1,0:T(8,128)(2,1)}), bf16[64,8,4096]{2,1,0:T(8,128)(2,1)}, u32[]{:S(2)}, u32[]{:S(2)}) async-start(bf16[64,8,4096]{2,1,0:T(8,128)(2,1)} %bitcast.129), calls=%async_computation.3 | async-start | bytes 8388608 | tf_op jit(solution)/shard_map/all_to_all | solution.py:50
  507.5 0.3 slice_reduce_fusion.1
  507.8 96.5 %all-to-all-done.1 = bf16[64,8,4096]{2,1,0:T(8,128)(2,1)} async-done(((bf16[64,8,4096]{2,1,0:T(8,128)(2,1)}), bf16[64,8,4096]{2,1,0:T(8,128)(2,1)}, u32[]{:S(2)}, u32[]{:S(2)}) %all-to-all-start.1) | async-done | bytes 4194336 | tf_op jit(solution)/shard_map/all_to_all | solution.py:50
  604.3 3.0 convolution_multiply_fusion.7
  607.3 3.0 fusion.8
  610.4 3.0 fusion.7
  613.5 3.0 fusion.6
  616.5 3.0 fusion.5
  619.6 3.1 fusion.4
  622.7 3.2 fusion.3
  625.9 3.8 fusion.9
  (23 shorter events, 0.1 us)
Async XLA Ops:
  6.5 312.5 %copy-start = (bf16[1,192,4096]{2,1,0:T(8,128)(2,1)S(1)}, bf16[1,192,4096]{2,1,0:T(8,128)(2,1)}, u32[]{:S(2)}) copy-start(bf16[1,192,4096]{2,1,0:T(8,128)(2,1)} %param.15) | copy-start | bytes 4718596
  6.5 6.3 copy-start.5
  6.5 6.6 %copy-start.4 = (bf16[4096]{0:T(1024)(128)(2,1)S(1)}, bf16[4096]{0:T(1024)(128)(2,1)}, u32[]{:S(2)}) copy-start(bf16[4096]{0:T(1024)(128)(2,1)} %param.11) | copy-start | bytes 24580
  6.5 39.7 %copy-start.3 = (bf16[32,4096]{1,0:T(8,128)(2,1)S(1)}, bf16[32,4096]{1,0:T(8,128)(2,1)}, u32[]{:S(2)}) copy-start(bf16[32,4096]{1,0:T(8,128)(2,1)} %param.10) | copy-start | bytes 786436
  6.5 39.7 %reduce-scatter.3.cloned.1.call-start = ((), (), s32[]{:S(2)}) async-start(), calls=%async_computation.4 | async-start | bytes 2621440 | tf_op jit(solution)/shard_map/reduce_scatter | solution.py:14
  12.8 294.0 %all-gather.3.cloned.1.call-start = ((), (), s32[]{:S(2)}) async-start(), calls=%async_computation.6 | async-start | bytes 20971520 | tf_op jit(solution)/shard_map/all_gather | solution.py:37
  159.5 335.0 %reduce-scatter.5.cloned.1.call-start = ((), (), s32[]{:S(2)}) async-start(), calls=%async_computation.5 | async-start | bytes 20971520 | tf_op jit(solution)/shard_map/reduce_scatter | solution.py:46
  494.6 13.3 %copy-start.6 = (f32[32,8]{0,1:T(8,128)S(1)}, f32[32,8]{0,1:T(8,128)}, u32[]{:S(2)}) copy-start(f32[32,8]{0,1:T(8,128)} %param.13) | copy-start | bytes 3076
  494.6 109.7 %all-to-all-start.1 = ((bf16[64,8,4096]{2,1,0:T(8,128)(2,1)}), bf16[64,8,4096]{2,1,0:T(8,128)(2,1)}, u32[]{:S(2)}, u32[]{:S(2)}) async-start(bf16[64,8,4096]{2,1,0:T(8,128)(2,1)} %bitcast.129), calls=%async_computation.3 | async-start | bytes 8388608 | tf_op jit(solution)/shard_map/all_to_all | solution.py:50
  619.6 6.3 copy-start.2
  622.7 7.0 %copy-start.1 = (bf16[1,192,4096]{2,1,0:T(8,128)(2,1)S(1)}, bf16[1,192,4096]{2,1,0:T(8,128)(2,1)}, u32[]{:S(2)}) copy-start(bf16[1,192,4096]{2,1,0:T(8,128)(2,1)} %param.15) | copy-start | bytes 4718596
Sparse Core Ops, SparseCore 0:
  12.9 33.2 reduce-scatter.2
  159.7 147.1 all-gather.2
  343.0 151.5 reduce-scatter.4
where the time goes:
time: 637 us; the launch traced here: 636 us
  waiting for transfers between devices  427 us (67%)
  blocking collectives  110 us (17%)
  matrix products  69.8 us (11%)
  between operations  13.3 us (2%)
  starting transfers between devices  13.2 us (2%)
    reduce_scatter x1, waiting for transfers between devices, local(): lax.psum_scatter(partials.astype(jnp.bfloat16), 'tp', scatter_dimension=0...  152 us
    all_gather x1, waiting for transfers between devices, local(): piece = lax.all_gather(received[None], 'tp', axis=0, tiled=True)  147 us
    all_to_all x1, blocking collectives, local(): lax.all_to_all(send_rows, 'ep', split_axis=0, concat_axis=0, tiled=True)  110 us
    all_to_all x1, waiting for transfers between devices, local(): lax.all_to_all(expert_out.reshape(ep_size, exp_local * capacity, model_wi...  96.5 us
    reduce_scatter x1, waiting for transfers between devices, local(): lax.psum_scatter(jnp.dot(context, wo_proj, preferred_element_type=jnp.flo...  31.8 us
    dot_general x8, matrix products, local(): picked = jnp.dot(picker, returned, preferred_element_type=jnp.float32)  25.3 us
    dot_general x1, matrix products, local(): jnp.einsum('nsjcf,jfd->nsjcd', activated, w_down, preferred_element_type=...  23.8 us
    all_to_all x1, starting transfers between devices, local(): lax.all_to_all(expert_out.reshape(ep_size, exp_local * capacity, model_wi...  12.9 us
  transfers between devices with their start and end apart: 4, of which 4 were waited for; matrix products, arithmetic and copies ran while one was open for 0% of the time, Pallas kernels for 0%

commit v1 on v0

--- a/solution.py
+++ b/solution.py
@@ -34,7 +34,9 @@
     send_rows = send_rows.reshape(ep_size, exp_local * capacity, model_width)
     received = lax.all_to_all(send_rows, "ep", split_axis=0, concat_axis=0, tiled=True)
     received = received.reshape(ep_size, exp_local, capacity, model_width)
-    piece = lax.all_gather(received[None], "tp", axis=0, tiled=True)
+    piece = jnp.concatenate(
+        lax.all_to_all(jnp.stack([received[None]] * lax.axis_size("tp")), "tp", 0, 0), axis=0
+    )
     gate = jnp.einsum(
         "nsjcd,jfd->nsjcf", piece, w_gate_up[:, 0], preferred_element_type=jnp.float32
     )

time: 637 us -> 672 us (1.055)
  blocking collectives: 110 us -> 297 us
  waiting for transfers between devices: 427 us -> 273 us
    all_to_all x0 -> x1, blocking collectives: none -> 187 us  [local(): lax.all_to_all(jnp.stack([received[None]] * lax.axis_size('tp')), 'tp', 0...]
    all_gather x1 -> x0, waiting for transfers between devices: 147 us -> none  [local(): piece = lax.all_gather(received[None], 'tp', axis=0, tiled=True)]
    reduce_scatter x1, waiting for transfers between devices: 152 us -> 144 us  [local(): lax.psum_scatter(partials.astype(jnp.bfloat16), 'tp', scatter_dimension=0...]
  transfers between devices with their start and end apart: 4 -> 3, of which waited for: 4 -> 3; matrix products, arithmetic and copies ran while one was open for 0% -> 0% of each run, Pallas kernels for 0% -> 0%
where the time goes in v1:
time: 672 us; the launch traced here: 671 us
  blocking collectives  297 us (44%)
  waiting for transfers between devices  273 us (41%)
  matrix products  69.8 us (10%)
  between operations  13.6 us (2%)
  starting transfers between devices  13 us (2%)
    all_to_all x1, blocking collectives, local(): lax.all_to_all(jnp.stack([received[None]] * lax.axis_size('tp')), 'tp', 0...  187 us
    reduce_scatter x1, waiting for transfers between devices, local(): lax.psum_scatter(partials.astype(jnp.bfloat16), 'tp', scatter_dimension=0...  144 us
    all_to_all x1, blocking collectives, local(): lax.all_to_all(send_rows, 'ep', split_axis=0, concat_axis=0, tiled=True)  110 us
    all_to_all x1, waiting for transfers between devices, local(): lax.all_to_all(expert_out.reshape(ep_size, exp_local * capacity, model_wi...  96.5 us
    reduce_scatter x1, waiting for transfers between devices, local(): lax.psum_scatter(jnp.dot(context, wo_proj, preferred_element_type=jnp.flo...  31.8 us
    dot_general x8, matrix products, local(): picked = jnp.dot(picker, returned, preferred_element_type=jnp.float32)  25.2 us
    dot_general x1, matrix products, local(): jnp.einsum('nsjcf,jfd->nsjcd', activated, w_down, preferred_element_type=...  23.8 us
  transfers between devices with their start and end apart: 3, of which 3 were waited for; matrix products, arithmetic and copies ran while one was open for 0% of the time, Pallas kernels for 0%

profile of v1, /device:TPU:32, one launch (start us, length us, event | category | flops | bytes accessed | tf_op | source)
XLA Modules:
  0.0 671.0 jit_solution(5180338689358919531)
XLA Ops:
  6.5 0.0 reduce-scatter.3.cloned.1.call-start
  6.6 6.2 fusion.59
  12.8 0.0 reduce-scatter.5.cloned.1.call-start
  12.9 0.1 copy.22
  12.9 0.1 eq.164
  13.0 0.1 eq.160
  13.2 0.6 reduce-window.6
  13.8 0.2 slice_reduce_fusion
  14.0 0.1 fusion.48
  14.1 0.1 reduce_sum.21
  14.2 0.2 fusion.43
  14.5 31.8 %reduce-scatter.3.cloned.1.call-done = f32[32,4096]{1,0:T(8,128)} async-done(((f32[128,4096]{1,0:T(8,128)}), f32[32,4096]{1,0:T(8,128)}) %reduce-scatter.3.cloned.1.call-update) | async-done | bytes 524304 | tf_op jit(solution)/shard_map/reduce_scatter | solution.py:14
  46.2 1.2 multiply_reduce_fusion
  47.5 2.4 fusion.4
  49.8 109.6 %all_to_all.15 = bf16[64,8,4096]{2,1,0:T(8,128)(2,1)S(1)} all-to-all(bf16[64,8,4096]{2,1,0:T(8,128)(2,1)S(1)} %fusion.4), channel_id=1, replica_groups=mesh['ep'=64,'tp'=4] {'ep'}, dimensions={0} | all-to-all | bytes 8388608 | tf_op jit(solution)/shard_map/all_to_all | solution.py:35
  159.4 2.1 stack.3
  161.5 187.3 %all_to_all.16 = bf16[4,1,64,1,8,4096]{5,4,2,3,1,0:T(8,128)(2,1)} all-to-all(bf16[4,1,64,1,8,4096]{5,4,2,3,1,0:T(8,128)(2,1)S(1)} %stack.3), channel_id=1, replica_groups=mesh['ep'=64,'tp'=4] {'tp'}, dimensions={0} | all-to-all | bytes 33554432 | tf_op jit(solution)/shard_map/all_to_all | solution.py:38
  348.8 12.2 %fusion = f32[4,64,8,192]{3,2,1,0:T(8,128)} fusion(bf16[4,1,64,1,8,4096]{5,4,2,3,1,0:T(8,128)(2,1)} %all_to_all.16, bf16[1,2,192,4096]{3,2,1,0:T(8,128)(2,1)} %param.14), kind=kOutput, calls=%fused_computation | convolution fusion | flops 3221225472 | bytes 19922944 | tf_op jit(solution)/shard_map/nsjcd,jfd->nsjcf/dot_general | solution.py:43
  361.0 23.8 %convert_bitcast_fusion = bf16[4,64,1,8,4096]{4,3,1,0,2:T(8,128)(2,1)} fusion(bf16[1,192,4096]{2,1,0:T(8,128)(2,1)S(1)} %copy-done, f32[4,64,8,192]{3,2,1,0:T(8,128)} %fusion, bf16[1,2,192,4096]{3,2,1,0:T(8,128)(2,1)} %param.14, bf16[4,1,64,1,8,4096]{5,4,2,3,1,0:T(8,128)(2,1)} %all_to_all.16), kind=kOutput, calls=%fused_computation.4 | convolution fusion | flops 6453198848 | bytes 38797312 | tf_op jit(solution)/shard_map/nsjcf,jfd->nsjcd/dot_general | solution.py:47
  384.8 0.0 reduce-scatter.5.cloned.1.call-update
  384.9 144.3 %reduce-scatter.5.cloned.1.call-done = bf16[1,64,1,8,4096]{4,3,1,0,2:T(8,128)(2,1)} async-done(((bf16[4,64,1,8,4096]{4,3,1,0,2:T(8,128)(2,1)}), bf16[1,64,1,8,4096]{4,3,1,0,2:T(8,128)(2,1)}) %reduce-scatter.5.cloned.1.call-update) | async-done | bytes 4194320 | tf_op jit(solution)/shard_map/reduce_scatter | solution.py:48
  529.2 12.9 %all-to-all-start.2 = ((bf16[64,8,4096]{2,1,0:T(8,128)(2,1)}), bf16[64,8,4096]{2,1,0:T(8,128)(2,1)}, u32[]{:S(2)}, u32[]{:S(2)}) async-start(bf16[64,8,4096]{2,1,0:T(8,128)(2,1)} %bitcast.137), calls=%async_computation.4 | async-start | bytes 8388608 | tf_op jit(solution)/shard_map/all_to_all | solution.py:52
  542.1 0.3 slice_reduce_fusion.1
  542.4 96.5 %all-to-all-done.2 = bf16[64,8,4096]{2,1,0:T(8,128)(2,1)} async-done(((bf16[64,8,4096]{2,1,0:T(8,128)(2,1)}), bf16[64,8,4096]{2,1,0:T(8,128)(2,1)}, u32[]{:S(2)}, u32[]{:S(2)}) %all-to-all-start.2) | async-done | bytes 4194336 | tf_op jit(solution)/shard_map/all_to_all | solution.py:52
  638.9 3.0 convolution_multiply_fusion.7
  642.0 3.0 fusion.12
  645.0 3.0 fusion.11
  648.0 3.0 fusion.10
  651.1 3.0 fusion.9
  654.1 3.1 fusion.8
  657.2 3.2 fusion.7
  660.4 3.8 fusion.13
  (22 shorter events, 0.1 us)
Async XLA Ops:
  6.5 354.5 %copy-start = (bf16[1,192,4096]{2,1,0:T(8,128)(2,1)S(1)}, bf16[1,192,4096]{2,1,0:T(8,128)(2,1)}, u32[]{:S(2)}) copy-start(bf16[1,192,4096]{2,1,0:T(8,128)(2,1)} %param.15) | copy-start | bytes 4718596
  6.5 6.3 copy-start.5
  6.5 6.6 copy-start.4
  6.5 39.7 %copy-start.3 = (bf16[32,4096]{1,0:T(8,128)(2,1)S(1)}, bf16[32,4096]{1,0:T(8,128)(2,1)}, u32[]{:S(2)}) copy-start(bf16[32,4096]{1,0:T(8,128)(2,1)} %param.10) | copy-start | bytes 786436
  6.5 39.7 %reduce-scatter.3.cloned.1.call-start = ((), (), s32[]{:S(2)}) async-start(), calls=%async_computation.5 | async-start | bytes 2621440 | tf_op jit(solution)/shard_map/reduce_scatter | solution.py:14
  12.8 516.4 %reduce-scatter.5.cloned.1.call-start = ((), (), s32[]{:S(2)}) async-start(), calls=%async_computation.6 | async-start | bytes 20971520 | tf_op jit(solution)/shard_map/reduce_scatter | solution.py:48
  529.2 13.3 %copy-start.6 = (f32[32,8]{0,1:T(8,128)S(1)}, f32[32,8]{0,1:T(8,128)}, u32[]{:S(2)}) copy-start(f32[32,8]{0,1:T(8,128)} %param.13) | copy-start | bytes 3076
  529.2 109.7 %all-to-all-start.2 = ((bf16[64,8,4096]{2,1,0:T(8,128)(2,1)}), bf16[64,8,4096]{2,1,0:T(8,128)(2,1)}, u32[]{:S(2)}, u32[]{:S(2)}) async-start(bf16[64,8,4096]{2,1,0:T(8,128)(2,1)} %bitcast.137), calls=%async_computation.4 | async-start | bytes 8388608 | tf_op jit(solution)/shard_map/all_to_all | solution.py:52
  654.1 6.3 copy-start.2
  657.2 7.0 %copy-start.1 = (bf16[1,192,4096]{2,1,0:T(8,128)(2,1)S(1)}, bf16[1,192,4096]{2,1,0:T(8,128)(2,1)}, u32[]{:S(2)}) copy-start(bf16[1,192,4096]{2,1,0:T(8,128)(2,1)} %param.15) | copy-start | bytes 4718596
Sparse Core Ops, SparseCore 0:
  12.9 33.2 reduce-scatter.2
  385.0 144.1 reduce-scatter.4
